TPU v7x, 32 devices: a whole 2x2x4 slice. The times are simulated.
32 devices in a mesh: dp: 8 (over z, y), tensor: 4 (over x, core).
Axes of the slice: x: 2, y: 2, z: 4, core: 2. Of those that a mesh axis runs over, the one named last changes fastest.
Arguments:
- query_act: bfloat16 [8, 1024, 1024], P('dp', None, 'tensor'), may hold values from -6 to 6
- rotated_keys: bfloat16 [8, 1024, 256], P('dp'), may hold values from -6 to 6
- value_input: bfloat16 [8, 1024, 256], P('dp'), may hold values from -6 to 6
- grad_out: bfloat16 [8, 1024, 8192], P('dp', 'tensor'), may hold values from -6 to 6
- out_weight: bfloat16 [1024, 8192], P('tensor', 'dp'), may hold values from -0.1875 to 0.1875
- doc_lengths: int32 [8, 4], P('dp'), may hold values from 1 to 512, 1024 in all within a row
Outputs:
- query_grad: bfloat16 [8, 1024, 1024], P('dp', None, 'tensor')
- key_gradient: bfloat16 [8, 4, 512, 128], P('dp', 'tensor')
- value_gradient: bfloat16 [8, 4, 512, 128], P('dp', 'tensor')
- weight_grad: float32 [1024, 8192], P('tensor', 'dp')
All inputs are finite; a program needn't handle non-finite values.
Results may differ from a plain program's by a relative error of at most 0.015.
The roundings to bfloat16 on the way count: a program that leaves them out, or rounds other values in their place, can miss the bound.
Values may be sent and summed in bfloat16 or wider, within the bound.
A program may use at most 128 MiB of HBM per device.

v0:
```python
import jax
import jax.numpy as jnp
from jax import lax
from jax.sharding import PartitionSpec as P

HEAD_SIZE = 128


def swapped(value, axis, apart):
    mask = 2**apart
    pairs = [(source, source ^ mask) for source in range(lax.axis_size(axis))]
    return lax.ppermute(value, axis, pairs)


def shards(query_act, rotated_keys, value_input, grad_out, out_weight, doc_lengths):
    score_scale = HEAD_SIZE ** (-0.5)
    tensor_index = lax.axis_index("tensor")
    kv_group = tensor_index // 2
    own_half = tensor_index % 2
    seq_len = query_act.shape[1]
    head_count = query_act.shape[2] // HEAD_SIZE
    query_heads = query_act[0].reshape(seq_len, head_count, HEAD_SIZE).transpose(1, 0, 2)
    key_rows = lax.dynamic_slice_in_dim(rotated_keys[0], kv_group * HEAD_SIZE, HEAD_SIZE, 1)
    value_rows = lax.dynamic_slice_in_dim(value_input[0], kv_group * HEAD_SIZE, HEAD_SIZE, 1)
    doc_ends = jnp.cumsum(doc_lengths[0])
    positions = jnp.arange(seq_len, dtype=jnp.int32)
    doc_ids = jnp.sum((positions[:, None] >= doc_ends[None, :]).astype(jnp.int32), axis=1)
    block_rows = min(512, seq_len)
    block_count = seq_len // block_rows
    full_weight = lax.all_gather(out_weight, "dp", axis=1, tiled=True)

    def key_reach():
        return seq_len

    def masked_scores(block_idx, key_span):
        first = block_idx * block_rows
        query_block = query_heads[:, first : first + block_rows]
        scores = (
            jnp.einsum("hqd,kd->hqk", query_block, key_rows, preferred_element_type=jnp.float32)
            * score_scale
        )
        allowed = (positions[None, :key_span] <= positions[first : first + block_rows, None]) & (
            doc_ids[None, :key_span] == doc_ids[first : first + block_rows, None]
        )
        return jnp.where(allowed[None], scores, -jnp.inf)

    totals_list = []
    outputs_list = []
    for block_idx in range(block_count):
        key_span = key_reach()
        scores = masked_scores(block_idx, key_span)
        row_max = jnp.max(scores, axis=-1, keepdims=True)
        log_total = row_max + jnp.log(jnp.sum(jnp.exp(scores - row_max), axis=-1, keepdims=True))
        prob_bf16 = jnp.exp(scores - log_total).astype(jnp.bfloat16)
        outputs_list.append(
            jnp.einsum(
                "hqk,kd->hqd", prob_bf16, value_rows, preferred_element_type=jnp.float32
            ).astype(jnp.bfloat16)
        )
        totals_list.append(log_total)
    attn_out = jnp.concatenate(outputs_list, axis=1)
    out_flat = attn_out.transpose(1, 0, 2).reshape(seq_len, head_count * HEAD_SIZE)
    local_rows = grad_out[0]
    gathered = lax.all_gather(local_rows, "tensor", axis=0, tiled=True)
    out_grad = jnp.einsum(
        "sd,hd->sh", gathered, full_weight, preferred_element_type=jnp.float32
    ).astype(jnp.bfloat16)
    weight_part = jnp.einsum("sh,sd->hd", out_flat, gathered, preferred_element_type=jnp.float32)
    weight_grad = lax.psum_scatter(weight_part, "dp", scatter_dimension=1, tiled=True)
    grad_heads = out_grad.reshape(seq_len, head_count, HEAD_SIZE).transpose(1, 0, 2)
    key_accum = jnp.zeros((seq_len, HEAD_SIZE), jnp.float32)
    value_accum = jnp.zeros((seq_len, HEAD_SIZE), jnp.float32)
    query_list = []
    for block_idx in range(block_count):
        key_span = key_reach()
        first = block_idx * block_rows
        scores = masked_scores(block_idx, key_span)
        prob_block = jnp.exp(scores - totals_list[block_idx])
        prob_bf16 = prob_block.astype(jnp.bfloat16)
        grad_block = grad_heads[:, first : first + block_rows]
        out_block = attn_out[:, first : first + block_rows]
        query_block = query_heads[:, first : first + block_rows]
        dprobs = jnp.einsum(
            "hqd,kd->hqk", grad_block, value_rows, preferred_element_type=jnp.float32
        )
        row_delta = jnp.sum(
            grad_block.astype(jnp.float32) * out_block.astype(jnp.float32), axis=-1, keepdims=True
        )
        score_gradient = (prob_block * (dprobs - row_delta) * score_scale).astype(jnp.bfloat16)
        query_list.append(
            jnp.einsum(
                "hqk,kd->hqd", score_gradient, key_rows, preferred_element_type=jnp.float32
            ).astype(jnp.bfloat16)
        )
        key_accum = key_accum.at[:key_span].add(
            jnp.einsum(
                "hqk,hqd->kd", score_gradient, query_block, preferred_element_type=jnp.float32
            )
        )
        value_accum = value_accum.at[:key_span].add(
            jnp.einsum("hqk,hqd->kd", prob_bf16, grad_block, preferred_element_type=jnp.float32)
        )
    query_grad = (
        jnp.concatenate(query_list, axis=1)
        .transpose(1, 0, 2)
        .reshape(1, seq_len, head_count * HEAD_SIZE)
    )
    half_rows = seq_len // 2
    other_start = (1 - own_half) * half_rows
    outgoing = (
        lax.dynamic_slice_in_dim(key_accum, other_start, half_rows, 0),
        lax.dynamic_slice_in_dim(value_accum, other_start, half_rows, 0),
    )
    partner = swapped((outgoing[0], outgoing[1]), "tensor", 0)
    key_mine = lax.dynamic_slice_in_dim(key_accum, own_half * half_rows, half_rows, 0) + partner[0]
    value_mine = (
        lax.dynamic_slice_in_dim(value_accum, own_half * half_rows, half_rows, 0) + partner[1]
    )
    key_gradient = key_mine.astype(jnp.bfloat16).reshape(1, 1, half_rows, HEAD_SIZE)
    value_gradient = value_mine.astype(jnp.bfloat16).reshape(1, 1, half_rows, HEAD_SIZE)
    return (query_grad, key_gradient, value_gradient, weight_grad)


def solution(mesh):
    placed = (
        P("dp", None, "tensor"),
        P("dp", None, None),
        P("dp", None, None),
        P("dp", "tensor", None),
        P("tensor", "dp"),
        P("dp", None),
    )
    return jax.shard_map(
        shards,
        mesh=mesh,
        in_specs=placed,
        out_specs=(
            P("dp", None, "tensor"),
            P("dp", "tensor", None, None),
            P("dp", "tensor", None, None),
            P("tensor", "dp"),
        ),
        check_vma=False,
    )
```

profile of v0, /device:TPU:0, one launch (start us, length us, event | category | flops | bytes accessed | tf_op | source)
XLA Modules:
  0.0 374.6 jit_solution(8681585686457070649)
XLA Ops:
  7.3 0.7 all-gather.4.cloned.1.call-update
  8.0 0.7 all-gather.6.cloned.1.call-update
  9.2 0.3 copy.30
  9.6 0.9 fusion.9
  10.5 0.9 fusion.7
  11.4 0.9 fusion.6
  12.4 2.2 exponential_reduce_fusion
  14.7 1.6 convolution_convert_fusion.1
  16.2 69.5 %all-gather.4.cloned.1.call-done = bf16[256,8192]{1,0:T(8,128)(2,1)} async-done(((bf16[256,1024]{1,0:T(8,128)(2,1)}), bf16[256,8192]{1,0:T(8,128)(2,1)}) %all-gather.4.cloned.1.call-update) | async-done | bytes 4194320 | tf_op jit(solution)/shard_map/all_gather | solution.py:30
  85.7 106.0 %all-gather.6.cloned.1.call-done = bf16[1,1024,8192]{2,1,0:T(8,128)(2,1)} async-done(((bf16[1,256,8192]{2,1,0:T(8,128)(2,1)}), bf16[1,1024,8192]{2,1,0:T(8,128)(2,1)}) %all-gather.6.cloned.1.call-update) | async-done | bytes 16777232 | tf_op jit(solution)/shard_map/all_gather | solution.py:64
  191.8 11.5 %fusion.10 = bf16[1024,256]{0,1:T(8,128)(2,1)S(1)} fusion(bf16[256,8192]{1,0:T(8,128)(2,1)} %all-gather.4.cloned.1.call-done, bf16[1,1024,8192]{2,1,0:T(8,128)(2,1)} %all-gather.6.cloned.1.call-done), kind=kOutput, calls=%fused_computation.20 | convolution fusion | flops 4295229440 | bytes 21495808 | tf_op jit(solution)/shard_map/sd,hd->sh/dot_general | solution.py:65
  203.2 0.3 copy.31
  203.5 3.8 %multiply_reduce_fusion.1 = (f32[2,512]{1,0:T(2,128)S(1)}, f32[2,512]{1,0:T(2,128)S(1)}, bf16[2,512,128]{2,1,0:T(8,128)(2,1)S(1)}) fusion(bf16[2,1024,128]{2,1,0:T(8,128)(2,1)S(1)} %bitcast.100, bf16[2,512,128]{2,1,0:T(8,128)(2,1)S(1)} %convolution_convert_fusion.1, bf16[1,1024,256]{2,1,0:T(8,128)(2,1)S(1)} %copy-done, s32[]{:T(128)S(6)} %select_n.33, ...), kind=kOutput, calls=%fused_computation.34 | convolution fusion | flops 273807360 | bytes 6041604 | tf_op jit(solution)/shard_map/hqk,kd->hqd/dot_general | solution.py:56
  207.4 0.2 copy.39
  207.6 12.5 %fusion = f32[256,8192]{1,0:T(8,128)} fusion(bf16[1024,256]{0,1:T(8,128)(2,1)S(1)} %bitcast.93, bf16[1,1024,8192]{2,1,0:T(8,128)(2,1)} %all-gather.6.cloned.1.call-done), kind=kOutput, calls=%fused_computation | convolution fusion | flops 4294967296 | bytes 25690112 | tf_op jit(solution)/shard_map/sh,sd->hd/dot_general | solution.py:68
  220.1 1.0 copy-done.7
  221.1 4.0 %multiply_convert_fusion = bf16[2,512,1024]{1,2,0:T(8,128)(2,1)S(1)} fusion(f32[1024,2,512]{2,0,1:T(8,128)} %copy-done.1, f32[2,512]{1,0:T(2,128)S(1)} %get-tuple-element.93, f32[2,512]{1,0:T(2,128)S(1)} %log_add_fusion, pred[512,1024]{0,1:T(8,128)(4,1)S(1)} %get-tuple-element.94, bf16[2,1024,128]{2,1,0:T(8,128)(2,1)S(1)} %bitcast.101, ...), kind=kOutput, calls=%fused_computation.6 | convolution fusion | flops 275775488 | bytes 7348228 | tf_op jit(solution)/shard_map/hqd,kd->hqk/dot_general | solution.py:83
  225.1 0.7 convolution_bitcast_fusion.2
  225.8 1.7 multiply_convert_fusion.1
  227.5 0.7 fusion.13
  228.3 0.3 collective-permute-start
  228.6 0.8 convolution_convert_fusion
  229.4 0.4 copy-done.2
  229.8 1.1 convolution_bitcast_fusion
  230.8 1.3 fusion.14
  232.1 0.8 convolution_convert_fusion.2
  232.9 0.3 collective-permute-start.1
  233.3 0.2 copy.38
  233.5 1.0 copy.40
  234.5 0.7 fusion.41
  235.2 1.6 fusion.42
  236.8 131.3 %reduce-scatter.2.cloned.1.call-done = f32[256,1024]{1,0:T(8,128)} async-done(((f32[256,8192]{1,0:T(8,128)}), f32[256,1024]{1,0:T(8,128)}) %reduce-scatter.2.cloned.1.call-update) | async-done | bytes 1048592 | tf_op jit(solution)/shard_map/reduce_scatter | solution.py:69
  (40 shorter events, 0.9 us)
Async XLA Ops:
  7.2 7.5 %copy-start = (bf16[1,1024,256]{2,1,0:T(8,128)(2,1)S(1)}, bf16[1,1024,256]{2,1,0:T(8,128)(2,1)}, u32[]{:S(2)}) copy-start(bf16[1,1024,256]{2,1,0:T(8,128)(2,1)} %param.24) | copy-start | bytes 1572868
  7.2 1.6 copy-start.10
  7.2 1.8 copy-start.5
  7.2 3.3 copy-start.8
  7.2 78.5 %all-gather.4.cloned.1.call-start = ((), (), s32[]{:S(2)}) async-start(), calls=%async_computation.1 | async-start | bytes 4718592 | tf_op jit(solution)/shard_map/all_gather | solution.py:30
  7.9 183.8 %all-gather.6.cloned.1.call-start = ((), (), s32[]{:S(2)}) async-start(), calls=%async_computation.3 | async-start | bytes 20971520 | tf_op jit(solution)/shard_map/all_gather | solution.py:64
  8.7 359.4 %reduce-scatter.2.cloned.1.call-start = ((), (), s32[]{:S(2)}) async-start(), calls=%async_computation.2 | async-start | bytes 9437184 | tf_op jit(solution)/shard_map/reduce_scatter | solution.py:69
  11.4 3.2 copy-start.1
  12.4 2.3 copy-start.3
  203.5 3.8 %copy-start.6 = (bf16[1024,2,128]{2,0,1:T(8,128)(2,1)}, bf16[1024,2,128]{2,0,1:T(8,128)(2,1)S(1)}, u32[]{:S(2)}) copy-start(bf16[1024,2,128]{2,0,1:T(8,128)(2,1)S(1)} %copy.31) | copy-start | bytes 1572868
  220.1 1.0 copy-start.7
  221.1 4.7 %copy-start.4 = (f32[1024,2,512]{2,0,1:T(8,128)S(1)}, f32[1024,2,512]{2,0,1:T(8,128)}, u32[]{:S(2)}) copy-start(f32[1024,2,512]{2,0,1:T(8,128)} %copy-done.3) | copy-start | bytes 12582916
  225.8 2.8 copy-start.9
  227.5 2.3 copy-start.2
  228.3 6.2 %collective-permute-start = (f32[512,128]{1,0:T(8,128)S(1)}, f32[512,128]{1,0:T(8,128)S(1)}, u32[]{:S(2)}, u32[]{:S(2)}) collective-permute-start(f32[512,128]{1,0:T(8,128)S(1)} %constant_dynamic-slice_fusion.1), channel_id=1, source_target_pairs={{0,1},{1,0},{2,3},{3,2},{4,5},{5,4},{6,7},{7,6},{8,9},{9,8},{10,11... | collective-permute-start | bytes 786440 | tf_op jit(solution)/shard_map/ppermute | solution.py:12
  232.9 2.3 collective-permute-start.1
Sparse Core Ops, SparseCore 0:
  10.2 75.4 all-gather.3
  87.3 104.4 all-gather.5
  220.2 147.8 reduce-scatter.1
where the time goes:
time: 375 us
  waiting for transfers between devices  308 us (82%)
  matrix products  42.1 us (11%)
  between operations  14.1 us (4%)
  other arithmetic  5.72 us (2%)
  local copies, waits for them, and re-layouts  3.8 us (1%)
    reduce_scatter x1, waiting for transfers between devices, shards(): lax.psum_scatter(weight_part, 'dp', scatter_dimension=1, tiled=True)  131 us
    all_gather x1, waiting for transfers between devices, shards(): gathered = lax.all_gather(local_rows, 'tensor', axis=0, tiled=True)  106 us
    all_gather x1, waiting for transfers between devices, shards(): full_weight = lax.all_gather(out_weight, 'dp', axis=1, tiled=True)  69.5 us
    dot_general x1, matrix products, shards(): jnp.einsum('sh,sd->hd', out_flat, gathered, preferred_element_type=jnp.fl...  12.5 us
    dot_general x1, matrix products, shards(): jnp.einsum('sd,hd->sh', gathered, full_weight, preferred_element_type=jnp...  11.5 us
  transfers between devices with their start and end apart: 5, of which 3 were waited for; matrix products, arithmetic and copies ran while one was open for 6% of the time, Pallas kernels for 0%

commit v1 on v0

--- a/solution.py
+++ b/solution.py
@@ -4,6 +4,22 @@
 from jax.sharding import PartitionSpec as P
 
 HEAD_SIZE = 128
+
+
+def ring_product(x, axis, dim, term):
+    length, position, width = (lax.axis_size(axis), lax.axis_index(axis), x.shape[dim])
+    forward = [(i, (i + 1) % length) for i in range(length)]
+    behind = [(i, (i - 1) % length) for i in range(length)]
+    half = length // 2
+    from_left = from_right = x
+    running = term(x, position * width)
+    for turn in range(1, half + 1):
+        from_left = lax.ppermute(from_left, axis, forward)
+        if turn < length - half:
+            from_right = lax.ppermute(from_right, axis, behind)
+            running = running + term(from_right, (position + turn) % length * width)
+        running = running + term(from_left, (position - turn) % length * width)
+    return running
 
 
 def swapped(value, axis, apart):
@@ -27,7 +43,6 @@
     doc_ids = jnp.sum((positions[:, None] >= doc_ends[None, :]).astype(jnp.int32), axis=1)
     block_rows = min(512, seq_len)
     block_count = seq_len // block_rows
-    full_weight = lax.all_gather(out_weight, "dp", axis=1, tiled=True)
 
     def key_reach():
         return seq_len
@@ -62,8 +77,16 @@
     out_flat = attn_out.transpose(1, 0, 2).reshape(seq_len, head_count * HEAD_SIZE)
     local_rows = grad_out[0]
     gathered = lax.all_gather(local_rows, "tensor", axis=0, tiled=True)
-    out_grad = jnp.einsum(
-        "sd,hd->sh", gathered, full_weight, preferred_element_type=jnp.float32
+    out_grad = ring_product(
+        out_weight,
+        "dp",
+        1,
+        lambda part, at: jnp.einsum(
+            "sd,hd->sh",
+            lax.dynamic_slice_in_dim(gathered, at, part.shape[1], axis=1),
+            part,
+            preferred_element_type=jnp.float32,
+        ),
     ).astype(jnp.bfloat16)
     weight_part = jnp.einsum("sh,sd->hd", out_flat, gathered, preferred_element_type=jnp.float32)
     weight_grad = lax.psum_scatter(weight_part, "dp", scatter_dimension=1, tiled=True)

time: 375 us -> 307 us (0.82)
  waiting for transfers between devices: 308 us -> 213 us
  starting transfers between devices: 0.76 us -> 20.4 us
  matrix products: 42.1 us -> 48.9 us
    all_gather x1, waiting for transfers between devices: 106 us -> 34.1 us  [shards(): gathered = lax.all_gather(local_rows, 'tensor', axis=0, tiled=True)]
    all_gather x1 -> x0, waiting for transfers between devices: 69.5 us -> none  [shards(): full_weight = lax.all_gather(out_weight, 'dp', axis=1, tiled=True)]
    ppermute x0 -> x7, waiting for transfers between devices: none -> 46.8 us  [the longest x4 46.8 us: ring_product(): from_left = lax.ppermute(from_left, axis, forward)]
    ppermute x0 -> x7, starting transfers between devices: none -> 19.7 us  [the longest x4 10.5 us: ring_product(): from_left = lax.ppermute(from_left, axis, forward)]
    dot_general x1 -> x8, matrix products: 11.5 us -> 15.8 us  [shards(): jnp.einsum('sd,hd->sh', lax.dynamic_slice_in_dim(gathered, at, part.shape...]
  transfers between devices with their start and end apart: 5 -> 11, of which waited for: 3 -> 5; matrix products, arithmetic and copies ran while one was open for 6% -> 12% of each run, Pallas kernels for 0% -> 0%
where the time goes in v1:
time: 307 us; the launch traced here: 306 us
  waiting for transfers between devices  213 us (69%)
  matrix products  48.9 us (16%)
  starting transfers between devices  20.4 us (7%)
  between operations  14.6 us (5%)
  other arithmetic  5.52 us (2%)
  local copies, waits for them, and re-layouts  3.72 us (1%)
    reduce_scatter x1, waiting for transfers between devices, shards(): lax.psum_scatter(weight_part, 'dp', scatter_dimension=1, tiled=True)  131 us
    ppermute x4, waiting for transfers between devices, ring_product(): from_left = lax.ppermute(from_left, axis, forward)  46.8 us
    all_gather x1, waiting for transfers between devices, shards(): gathered = lax.all_gather(local_rows, 'tensor', axis=0, tiled=True)  34.1 us
    dot_general x8, matrix products, shards(): jnp.einsum('sd,hd->sh', lax.dynamic_slice_in_dim(gathered, at, part.shape...  15.8 us
    dot_general x1, matrix products, shards(): jnp.einsum('sh,sd->hd', out_flat, gathered, preferred_element_type=jnp.fl...  12.7 us
    ppermute x4, starting transfers between devices, ring_product(): from_left = lax.ppermute(from_left, axis, forward)  10.5 us
    ppermute x3, starting transfers between devices, ring_product(): from_right = lax.ppermute(from_right, axis, behind)  9.23 us
    dot_general x2, matrix products, shards(): jnp.einsum('hqk,kd->hqd', prob_bf16, value_rows, preferred_element_type=j...  7.65 us
  transfers between devices with their start and end apart: 11, of which 5 were waited for; matrix products, arithmetic and copies ran while one was open for 12% of the time, Pallas kernels for 0%

profile of v1, /device:TPU:0, one launch (start us, length us, event | category | flops | bytes accessed | tf_op | source)
XLA Modules:
  0.0 306.1 jit_solution(13719683005017068003)
XLA Ops:
  8.0 3.0 collective-permute-start.1
  11.0 3.1 %collective-permute-start = (bf16[256,1024]{1,0:T(8,128)(2,1)}, bf16[256,1024]{1,0:T(8,128)(2,1)S(1)}, u32[]{:S(2)}, u32[]{:S(2)}) collective-permute-start(bf16[256,1024]{1,0:T(8,128)(2,1)} %param.26), channel_id=1, source_target_pairs={{0,28},{4,0},{8,4},{12,8},{16,12},{20,16},{24,20},{28,24},{1,29},{... | collective-permute-start | bytes 1572872 | tf_op jit(solution)/shard_map/ppermute | solution.py:19
  15.0 0.9 fusion.31
  15.9 0.9 fusion.5
  16.8 0.9 fusion.4
  17.8 16.0 %collective-permute-done.1 = bf16[256,1024]{1,0:T(8,128)(2,1)} collective-permute-done((bf16[256,1024]{1,0:T(8,128)(2,1)}, bf16[256,1024]{1,0:T(8,128)(2,1)}, u32[]{:S(2)}, u32[]{:S(2)}) %collective-permute-start.1) | collective-permute-done | bytes 524320 | tf_op jit(solution)/shard_map/ppermute | solution.py:17
  33.8 2.5 collective-permute-start.3
  36.3 2.0 exponential_reduce_fusion
  38.3 3.1 %collective-permute-start.2 = (bf16[256,1024]{1,0:T(8,128)(2,1)S(1)}, bf16[256,1024]{1,0:T(8,128)(2,1)S(1)}, u32[]{:S(2)}, u32[]{:S(2)}) collective-permute-start(bf16[256,1024]{1,0:T(8,128)(2,1)S(1)} %collective-permute-done), channel_id=1, source_target_pairs={{0,28},{4,0},{8,4},{12,8},{16,12},{20,16},{24,20},{28,24},{1,29},{... | collective-permute-start | bytes 1572872 | tf_op jit(solution)/shard_map/ppermute | solution.py:19
  41.4 16.8 %collective-permute-done.3 = bf16[256,1024]{1,0:T(8,128)(2,1)} collective-permute-done((bf16[256,1024]{1,0:T(8,128)(2,1)}, bf16[256,1024]{1,0:T(8,128)(2,1)}, u32[]{:S(2)}, u32[]{:S(2)}) %collective-permute-start.3) | collective-permute-done | bytes 524320 | tf_op jit(solution)/shard_map/ppermute | solution.py:17
  58.1 2.5 collective-permute-start.5
  60.8 3.9 %convolution_convert_fusion.1 = bf16[2,512,128]{2,1,0:T(8,128)(2,1)S(1)} fusion(bf16[1,1024,256]{2,1,0:T(8,128)(2,1)S(1)} %copy-done, s32[]{:T(128)S(6)} %select_n.85, f32[1024,2,512]{2,0,1:T(8,128)} %copy-done.2, f32[2,512]{1,0:T(2,128)S(1)} %log_add_fusion, pred[512,1024]{0,1:T(8,128)(4,1)S(1)} %get-tuple-element.94), kind=kOutput, calls=%fused_computation.57 | convolution fusion | flops 272760832 | bytes 5246980 | tf_op jit(solution)/shard_map/hqk,kd->hqd/dot_general | solution.py:71
  64.6 3.0 collective-permute-start.4
  67.7 14.0 %collective-permute-done.5 = bf16[256,1024]{1,0:T(8,128)(2,1)} collective-permute-done((bf16[256,1024]{1,0:T(8,128)(2,1)}, bf16[256,1024]{1,0:T(8,128)(2,1)}, u32[]{:S(2)}, u32[]{:S(2)}) %collective-permute-start.5) | collective-permute-done | bytes 524320 | tf_op jit(solution)/shard_map/ppermute | solution.py:17
  81.6 2.5 collective-permute-start.6
  84.1 34.1 %all-gather.3.cloned.1.call-done = bf16[1,1024,8192]{2,1,0:T(8,128)(2,1)} async-done(((bf16[1,256,8192]{2,1,0:T(8,128)(2,1)}), bf16[1,1024,8192]{2,1,0:T(8,128)(2,1)}) %all-gather.3.cloned.1.call-update) | async-done | bytes 16777232 | tf_op jit(solution)/shard_map/all_gather | solution.py:79
  118.2 2.6 fusion.12
  120.8 2.9 fusion.16
  123.8 3.1 %fusion.20 = f32[1024,256]{0,1:T(8,128)S(1)} fusion(bf16[256,1024]{1,0:T(8,128)(2,1)} %param.26, bf16[1,1024,8192]{2,1,0:T(8,128)(2,1)} %all-gather.3.cloned.1.call-done, s32[]{:T(128)S(6)} %select_n.87), kind=kOutput, calls=%fused_computation.28 | convolution fusion | flops 536870912 | bytes 3670020 | tf_op jit(solution)/shard_map/sd,hd->sh/dot_general | solution.py:84
  128.5 1.8 fusion.8
  130.4 1.9 fusion.47
  132.3 1.8 fusion.53
  134.4 3.8 %multiply_reduce_fusion.1 = (f32[2,512]{1,0:T(2,128)S(1)}, f32[2,512]{1,0:T(2,128)S(1)}, bf16[2,512,128]{2,1,0:T(8,128)(2,1)S(1)}) fusion(bf16[2,1024,128]{2,1,0:T(8,128)(2,1)S(1)} %bitcast.144, bf16[2,512,128]{2,1,0:T(8,128)(2,1)S(1)} %convolution_convert_fusion.1, bf16[1,1024,256]{2,1,0:T(8,128)(2,1)S(1)} %copy-done, s32[]{:T(128)S(6)} %select_n.85, ...), kind=kOutput, calls=%fused_computation.63 | convolution fusion | flops 273807360 | bytes 6041604 | tf_op jit(solution)/shard_map/hqk,kd->hqd/dot_general | solution.py:71
  138.5 12.7 %fusion = f32[256,8192]{1,0:T(8,128)} fusion(bf16[1024,256]{0,1:T(8,128)(2,1)S(1)} %bitcast.136, bf16[1,1024,8192]{2,1,0:T(8,128)(2,1)} %all-gather.3.cloned.1.call-done), kind=kOutput, calls=%fused_computation | convolution fusion | flops 4294967296 | bytes 25690112 | tf_op jit(solution)/shard_map/sh,sd->hd/dot_general | solution.py:91
  151.2 1.0 copy-done.8
  152.2 4.0 %multiply_convert_fusion = bf16[2,512,1024]{1,2,0:T(8,128)(2,1)S(1)} fusion(f32[1024,2,512]{2,0,1:T(8,128)} %copy-done.2, f32[2,512]{1,0:T(2,128)S(1)} %get-tuple-element.93, f32[2,512]{1,0:T(2,128)S(1)} %log_add_fusion, pred[512,1024]{0,1:T(8,128)(4,1)S(1)} %get-tuple-element.94, bf16[2,1024,128]{2,1,0:T(8,128)(2,1)S(1)} %bitcast.145, ...), kind=kOutput, calls=%fused_computation.4 | convolution fusion | flops 275775488 | bytes 7348228 | tf_op jit(solution)/shard_map/hqd,kd->hqk/dot_general | solution.py:106
  156.9 1.7 multiply_convert_fusion.1
  160.9 1.1 convolution_bitcast_fusion
  162.0 1.3 fusion.57
  164.6 1.0 copy.40
  165.6 1.6 fusion.84
  167.9 131.3 %reduce-scatter.2.cloned.1.call-done = f32[256,1024]{1,0:T(8,128)} async-done(((f32[256,8192]{1,0:T(8,128)}), f32[256,1024]{1,0:T(8,128)}) %reduce-scatter.2.cloned.1.call-update) | async-done | bytes 1048592 | tf_op jit(solution)/shard_map/reduce_scatter | solution.py:92
  (60 shorter events, 8.8 us)
Async XLA Ops:
  7.2 53.6 %copy-start = (bf16[1,1024,256]{2,1,0:T(8,128)(2,1)S(1)}, bf16[1,1024,256]{2,1,0:T(8,128)(2,1)}, u32[]{:S(2)}) copy-start(bf16[1,1024,256]{2,1,0:T(8,128)(2,1)} %param.24) | copy-start | bytes 1572868
  7.2 7.0 %copy-start.11 = (s32[1,4]{1,0:T(1,128)S(1)}, s32[1,4]{1,0:T(1,128)}, u32[]{:S(2)}) copy-start(s32[1,4]{1,0:T(1,128)} %param.27) | copy-start | bytes 52
  7.2 7.2 %copy-start.6 = (bf16[1,1024,256]{2,1,0:T(8,128)(2,1)S(1)}, bf16[1,1024,256]{2,1,0:T(8,128)(2,1)}, u32[]{:S(2)}) copy-start(bf16[1,1024,256]{2,1,0:T(8,128)(2,1)} %param.22) | copy-start | bytes 1572868
  7.2 8.7 %copy-start.9 = (bf16[1,1024,256]{2,1,0:T(8,128)(2,1)S(1)}, bf16[1,1024,256]{2,1,0:T(8,128)(2,1)}, u32[]{:S(2)}) copy-start(bf16[1,1024,256]{2,1,0:T(8,128)(2,1)} %param.23) | copy-start | bytes 1572868
  7.2 111.0 %all-gather.3.cloned.1.call-start = ((), (), s32[]{:S(2)}) async-start(), calls=%async_computation.2 | async-start | bytes 20971520 | tf_op jit(solution)/shard_map/all_gather | solution.py:79
  7.9 291.3 %reduce-scatter.2.cloned.1.call-start = ((), (), s32[]{:S(2)}) async-start(), calls=%async_computation.1 | async-start | bytes 9437184 | tf_op jit(solution)/shard_map/reduce_scatter | solution.py:92
  8.0 25.8 %collective-permute-start.1 = (bf16[256,1024]{1,0:T(8,128)(2,1)}, bf16[256,1024]{1,0:T(8,128)(2,1)}, u32[]{:S(2)}, u32[]{:S(2)}) collective-permute-start(bf16[256,1024]{1,0:T(8,128)(2,1)} %param.26), channel_id=1, source_target_pairs={{0,4},{4,8},{8,12},{12,16},{16,20},{20,24},{24,28},{28,0},{1,5},{5... | collective-permute-start | bytes 1572872 | tf_op jit(solution)/shard_map/ppermute | solution.py:17
  11.0 27.2 %collective-permute-start = (bf16[256,1024]{1,0:T(8,128)(2,1)}, bf16[256,1024]{1,0:T(8,128)(2,1)S(1)}, u32[]{:S(2)}, u32[]{:S(2)}) collective-permute-start(bf16[256,1024]{1,0:T(8,128)(2,1)} %param.26), channel_id=1, source_target_pairs={{0,28},{4,0},{8,4},{12,8},{16,12},{20,16},{24,20},{28,24},{1,29},{... | collective-permute-start | bytes 1572872 | tf_op jit(solution)/shard_map/ppermute | solution.py:19
  16.8 21.4 %copy-start.2 = (f32[1024,2,512]{2,0,1:T(8,128)}, f32[1024,2,512]{2,0,1:T(8,128)S(1)}, u32[]{:S(2)}) copy-start(f32[1024,2,512]{2,0,1:T(8,128)S(1)} %get-tuple-element.101) | copy-start | bytes 12582916
  17.8 20.5 %copy-start.4 = (f32[1024,2,512]{2,0,1:T(8,128)}, f32[1024,2,512]{2,0,1:T(8,128)S(1)}, u32[]{:S(2)}) copy-start(f32[1024,2,512]{2,0,1:T(8,128)S(1)} %get-tuple-element.99) | copy-start | bytes 12582916
  33.8 24.4 %collective-permute-start.3 = (bf16[256,1024]{1,0:T(8,128)(2,1)}, bf16[256,1024]{1,0:T(8,128)(2,1)}, u32[]{:S(2)}, u32[]{:S(2)}) collective-permute-start(bf16[256,1024]{1,0:T(8,128)(2,1)} %collective-permute-done.1), channel_id=1, source_target_pairs={{0,4},{4,8},{8,12},{12,16},{16,20},{20,24},{24,28},{28,0},{1,5},{5... | collective-permute-start | bytes 1572872 | tf_op jit(solution)/shard_map/ppermute | solution.py:17
  38.3 26.4 %collective-permute-start.2 = (bf16[256,1024]{1,0:T(8,128)(2,1)S(1)}, bf16[256,1024]{1,0:T(8,128)(2,1)S(1)}, u32[]{:S(2)}, u32[]{:S(2)}) collective-permute-start(bf16[256,1024]{1,0:T(8,128)(2,1)S(1)} %collective-permute-done), channel_id=1, source_target_pairs={{0,28},{4,0},{8,4},{12,8},{16,12},{20,16},{24,20},{28,24},{1,29},{... | collective-permute-start | bytes 1572872 | tf_op jit(solution)/shard_map/ppermute | solution.py:19
  58.1 23.5 %collective-permute-start.5 = (bf16[256,1024]{1,0:T(8,128)(2,1)}, bf16[256,1024]{1,0:T(8,128)(2,1)}, u32[]{:S(2)}, u32[]{:S(2)}) collective-permute-start(bf16[256,1024]{1,0:T(8,128)(2,1)} %collective-permute-done.3), channel_id=1, source_target_pairs={{0,4},{4,8},{8,12},{12,16},{16,20},{20,24},{24,28},{28,0},{1,5},{5... | collective-permute-start | bytes 1572872 | tf_op jit(solution)/shard_map/ppermute | solution.py:17
  64.6 65.7 %collective-permute-start.4 = (bf16[256,1024]{1,0:T(8,128)(2,1)S(1)}, bf16[256,1024]{1,0:T(8,128)(2,1)}, u32[]{:S(2)}, u32[]{:S(2)}) collective-permute-start(bf16[256,1024]{1,0:T(8,128)(2,1)S(1)} %collective-permute-done.2), channel_id=1, source_target_pairs={{0,28},{4,0},{8,4},{12,8},{16,12},{20,16},{24,20},{28,24},{1,29},{... | collective-permute-start | bytes 1572872 | tf_op jit(solution)/shard_map/ppermute | solution.py:19
  81.6 50.6 %collective-permute-start.6 = (bf16[256,1024]{1,0:T(8,128)(2,1)}, bf16[256,1024]{1,0:T(8,128)(2,1)}, u32[]{:S(2)}, u32[]{:S(2)}) collective-permute-start(bf16[256,1024]{1,0:T(8,128)(2,1)} %collective-permute-done.5), channel_id=1, source_target_pairs={{0,4},{4,8},{8,12},{12,16},{16,20},{20,24},{24,28},{28,0},{1,5},{5... | collective-permute-start | bytes 1572872 | tf_op jit(solution)/shard_map/ppermute | solution.py:17
  118.2 8.6 %copy-start.1 = (bf16[1,1024,8192]{2,1,0:T(8,128)(2,1)S(1)}, bf16[1,1024,8192]{2,1,0:T(8,128)(2,1)}, u32[]{:S(2)}) copy-start(bf16[1,1024,8192]{2,1,0:T(8,128)(2,1)} %all-gather.3.cloned.1.call-done) | copy-start | bytes 50331652
  134.4 3.8 %copy-start.7 = (bf16[1024,2,128]{2,0,1:T(8,128)(2,1)}, bf16[1024,2,128]{2,0,1:T(8,128)(2,1)S(1)}, u32[]{:S(2)}) copy-start(bf16[1024,2,128]{2,0,1:T(8,128)(2,1)S(1)} %copy.31) | copy-start | bytes 1572868
  151.2 1.0 copy-start.8
  152.2 4.7 %copy-start.5 = (f32[1024,2,512]{2,0,1:T(8,128)S(1)}, f32[1024,2,512]{2,0,1:T(8,128)}, u32[]{:S(2)}) copy-start(f32[1024,2,512]{2,0,1:T(8,128)} %copy-done.4) | copy-start | bytes 12582916
  156.9 2.8 copy-start.10
  158.6 2.3 copy-start.3
  159.4 6.2 %collective-permute-start.7 = (f32[512,128]{1,0:T(8,128)S(1)}, f32[512,128]{1,0:T(8,128)}, u32[]{:S(2)}, u32[]{:S(2)}) collective-permute-start(f32[512,128]{1,0:T(8,128)S(1)} %constant_dynamic-slice_fusion.1), channel_id=1, source_target_pairs={{0,1},{1,0},{2,3},{3,2},{4,5},{5,4},{6,7},{7,6},{8,9},{9,8},{10,11... | collective-permute-start | bytes 786440 | tf_op jit(solution)/shard_map/ppermute | solution.py:28
  164.0 3.2 %collective-permute-start.8 = (f32[512,128]{1,0:T(8,128)S(1)}, f32[512,128]{1,0:T(8,128)S(1)}, u32[]{:S(2)}, u32[]{:S(2)}) collective-permute-start(f32[512,128]{1,0:T(8,128)S(1)} %constant_dynamic-slice_fusion), channel_id=1, source_target_pairs={{0,1},{1,0},{2,3},{3,2},{4,5},{5,4},{6,7},{7,6},{8,9},{9,8},{10,11... | collective-permute-start | bytes 786440 | tf_op jit(solution)/shard_map/ppermute | solution.py:28
Sparse Core Ops, SparseCore 0:
  9.6 108.6 all-gather.2
  151.3 147.8 reduce-scatter.1
